TPU v7x, 768 devices: a whole 4x8x12 slice. The times are simulated.
768 devices in a mesh: pts: 64 (over y, x, core), bins: 12 (over z).
Axes of the slice: x: 4, y: 8, z: 12, core: 2. Of those that a mesh axis runs over, the one named last changes fastest.
Arguments:
- spectrum: bfloat16 [1296, 256, 1536], P('bins', 'pts'), may hold values from 0.049804688 to 4
- courant: float32 [1296, 2], replicated, may hold values from 0.05 to 0.45
- upwind: int32 [1296, 2], replicated, may hold values from 0 to 1
- coupling: bfloat16 [1296, 1296], replicated, may hold values from -0.15625 to 0.15625
- sea: int32 [256, 1536], P('pts'), may hold values 0 or 1
- owner: int32 [64, 12, 512, 1], P('pts', 'bins'), may hold values from 0 to 63; in each aligned block of 512 rows (0 to 511, 512 to 1023, ..., all dimensions but the last counted through in order) at most 16 rows name the same one
Outputs:
- owner_rows: bfloat16 [64, 12, 1024, 1296], P('pts', 'bins')
Inputs may be any that keep to these rules, and one draw needn't show every extreme that they name: Among the 512 points of one block, at most 16 name the same owner, and in every draw some owner is named by exactly 16 points of some block.
All inputs are finite; a program needn't handle non-finite values. No bound on the sum of `sea` on one device may be relied on, other than what follows from the above.
Results may differ from a plain program's by a relative error of at most 0.0049.
Values may be sent and summed in bfloat16 or wider, within the bound.
A program may use at most 32 MiB of HBM per device.

v0:
```python
import jax
import jax.numpy as jnp
from jax import lax
from jax.sharding import PartitionSpec as P


def padded_2(block, sides, width):
    for axis, dim in sides:
        count = lax.axis_size(axis)
        forward = [(i, i + 1) for i in range(count - 1)]
        backward = [(target, source) for source, target in forward]
        low = lax.ppermute(
            lax.slice_in_dim(block, block.shape[dim] - width, None, axis=dim), axis, forward
        )
        high = lax.ppermute(lax.slice_in_dim(block, 0, width, axis=dim), axis, backward)
        block = jnp.concatenate([low, block, high], axis=dim)
    return block


def advect(padded, sea_mask, courant, upwind):
    center = padded[:, 1:-1, 1:-1]
    donor_x = jnp.where(upwind[:, 0][:, None, None] == 0, padded[:, :-2, 1:-1], padded[:, 2:, 1:-1])
    donor_y = jnp.where(upwind[:, 1][:, None, None] == 0, padded[:, 1:-1, :-2], padded[:, 1:-1, 2:])
    moved = (
        center
        - courant[:, 0][:, None, None] * (center - donor_x)
        - courant[:, 1][:, None, None] * (center - donor_y)
    )
    return (moved * sea_mask[None]).astype(jnp.bfloat16)


def local(spectrum, courant, upwind, coupling, sea, owner):
    local_bins = spectrum.shape[0]
    lon_rows = spectrum.shape[1]
    bins_count = lax.axis_size("bins")
    lat_cells = spectrum.shape[2] // bins_count
    masked = spectrum * sea.astype(jnp.bfloat16)[None]
    local_sea = lax.dynamic_slice_in_dim(
        sea, lax.axis_index("bins") * lat_cells, lat_cells, 1
    ).astype(jnp.float32)
    first_bin = lax.axis_index("bins") * local_bins
    my_courant = lax.dynamic_slice_in_dim(courant, first_bin, local_bins, 0)
    my_upwind = lax.dynamic_slice_in_dim(upwind, first_bin, local_bins, 0)
    extended = padded_2(masked, (("pts", 1),), 1)
    extended = jnp.pad(extended.astype(jnp.float32), ((0, 0), (0, 0), (1, 1)))
    moved = advect(extended, sea.astype(jnp.float32), my_courant, my_upwind)
    columns = lax.all_to_all(moved, "bins", split_axis=2, concat_axis=0, tiled=True)
    all_bins = columns.shape[0]
    points = lon_rows * lat_cells
    flat = columns.reshape(all_bins, points)
    energy = jnp.mean(flat.astype(jnp.float32), axis=0)
    coupled = jnp.einsum("bp,bc->pc", flat, coupling, preferred_element_type=jnp.float32)
    weights = local_sea.reshape(points)
    updated = (
        weights[:, None] * (flat.astype(jnp.float32).T + coupled) / (1.0 + energy)[:, None]
    ).astype(jnp.bfloat16)
    owners_count = lax.axis_size("pts")
    capacity = max(2, (2 * points + owners_count - 1) // owners_count)
    target = owner.reshape(points)
    onehot = (target[:, None] == jnp.arange(owners_count, dtype=jnp.int32)[None, :]).astype(
        jnp.int32
    )
    slot_rank = jnp.sum(jnp.cumsum(onehot, axis=0) * onehot, axis=1) - 1
    slot_index = target * capacity + slot_rank
    selector = (
        slot_index[None, :] == jnp.arange(owners_count * capacity, dtype=jnp.int32)[:, None]
    ).astype(jnp.bfloat16)
    outgoing = jnp.dot(selector, updated, preferred_element_type=jnp.float32).astype(jnp.bfloat16)
    outgoing = outgoing.reshape(owners_count, capacity, all_bins)
    received = lax.all_to_all(outgoing, "pts", split_axis=0, concat_axis=0, tiled=True)
    return received.reshape(1, 1, owners_count * capacity, all_bins)


def solution(mesh):
    placed = (P("bins", "pts", None), P(), P(), P(), P("pts", None), P("pts", "bins", None, None))
    return jax.shard_map(
        local, mesh=mesh, in_specs=placed, out_specs=P("pts", "bins", None, None), check_vma=False
    )
```

profile of v0, /device:TPU:1, one launch (start us, length us, event | category | flops | bytes accessed | tf_op | source)
XLA Modules:
  0.0 188.4 jit_solution(5428893170767778364)
XLA Ops:
  0.0 0.8 fusion.21
  0.8 1.8 copy_multiply_fusion
  2.6 12.4 %collective-permute-start.1 = (bf16[108,1,1536]{2,0,1:T(8,128)(2,1)S(1)}, bf16[108,1,1536]{2,0,1:T(8,128)(2,1)S(1)}, u32[]{:S(2)}, u32[]{:S(2)}) collective-permute-start(bf16[108,1,1536]{2,0,1:T(8,128)(2,1)S(1)} %get-tuple-element.6), channel_id=1, source_target_pairs={{12,0},{24,12},{36,24},{48,36},{60,48},{72,60},{84,72},{96,84},{10... | collective-permute-start | bytes 995336 | tf_op jit(solution)/shard_map/ppermute | solution.py:15
  15.1 1.9 %collective-permute-start = (bf16[108,1,1536]{2,0,1:T(8,128)(2,1)S(1)}, bf16[108,1,1536]{2,0,1:T(8,128)(2,1)S(1)}, u32[]{:S(2)}, u32[]{:S(2)}) collective-permute-start(bf16[108,1,1536]{2,0,1:T(8,128)(2,1)S(1)} %get-tuple-element.5), channel_id=1, source_target_pairs={{0,12},{12,24},{24,36},{36,48},{48,60},{60,72},{72,84},{84,96},{96... | collective-permute-start | bytes 995336 | tf_op jit(solution)/shard_map/ppermute | solution.py:12
  17.0 0.1 constant_dynamic-slice_fusion.1
  17.1 0.8 constant_dynamic-slice_fusion
  17.9 3.3 %collective-permute-done = bf16[108,1,1536]{2,0,1:T(8,128)(2,1)S(1)} collective-permute-done((bf16[108,1,1536]{2,0,1:T(8,128)(2,1)S(1)}, bf16[108,1,1536]{2,0,1:T(8,128)(2,1)S(1)}, u32[]{:S(2)}, u32[]{:S(2)}) %collective-permute-start) | collective-permute-done | bytes 331808 | tf_op jit(solution)/shard_map/ppermute | solution.py:12
  21.2 0.3 maximum_convert_fusion
  21.5 2.1 %fusion.8 = bf16[108,4,1536]{2,0,1:T(8,128)(2,1)S(1)} fusion(f32[108,6,1536]{2,0,1:T(8,128)S(1)} %maximum_convert_fusion, f32[4,1536]{1,0:T(4,128)S(1)} %get-tuple-element.7, f32[108]{0:T(128)S(1)} %get-tuple-element.12, f32[108]{0:T(128)S(1)} %get-tuple-element.11, pred[108]{0:T(512)(128)(4,1)S(1)} %get-tuple-element.10, pred[108]{0:T(512)(128)(4,1)S(1)} %get-tuple-element.9), kind=kLoop, calls=%fused_computation.13 | loop fusion | flops 6635520 | bytes 13740032 | tf_op jit(solution)/shard_map/convert_element_type | solution.py:29
  23.7 0.0 copy-start.1
  23.7 2.3 %copy.21 = bf16[108,4,1536]{0,1,2:T(4,128)(2,1)} copy(bf16[108,4,1536]{2,0,1:T(8,128)(2,1)S(1)} %fusion.8) | data formatting | bytes 2654208 | tf_op jit(solution)/shard_map/convert_element_type | solution.py:29
  25.9 7.0 %all-to-all-start = ((bf16[108,4,1536]{0,1,2:T(4,128)(2,1)}), bf16[108,4,1536]{0,1,2:T(4,128)(2,1)S(1)}, u32[]{:S(2)}, u32[]{:S(2)}) async-start(bf16[108,4,1536]{0,1,2:T(4,128)(2,1)} %copy.21), calls=%async_computation | async-start | bytes 3145728 | tf_op jit(solution)/shard_map/all_to_all | solution.py:47
  32.9 1.2 reduce-window.6
  34.1 0.2 slice_reduce_fusion
  34.4 0.7 convert_bitcast_fusion
  35.1 0.1 fusion.18
  35.2 52.4 %all-to-all-done = bf16[108,4,1536]{0,1,2:T(4,128)(2,1)S(1)} async-done(((bf16[108,4,1536]{0,1,2:T(4,128)(2,1)}), bf16[108,4,1536]{0,1,2:T(4,128)(2,1)S(1)}, u32[]{:S(2)}, u32[]{:S(2)}) %all-to-all-start) | async-done | bytes 1327136 | tf_op jit(solution)/shard_map/all_to_all | solution.py:47
  87.6 0.2 copy.22
  87.8 1.1 copy.23
  88.9 0.4 convert_reduce_fusion
  89.2 7.4 %convolution_convert_fusion = bf16[1024,1296]{0,1:T(8,128)(2,1)} fusion(s32[512]{0:T(512)S(1)} %add_add_fusion, bf16[1296,1296]{1,0:T(8,128)(2,1)} %param.9, bf16[162,8,4,128]{3,2,1,0:T(4,128)(2,1)S(1)} %bitcast.50, f32[512]{0:T(512)S(1)} %add_bitcast_fusion.1, f32[512]{0:T(512)S(1)} %convert_bitcast_fusion), kind=kOutput, calls=%fused_computation.2 | convolution fusion | flops 3084050432 | bytes 7346688 | tf_op jit(solution)/shard_map/dot_general | solution.py:68
  96.6 3.3 %copy.24 = bf16[1024,1296]{1,0:T(8,128)(2,1)S(1)} copy(bf16[1024,1296]{0,1:T(8,128)(2,1)} %convolution_convert_fusion) | data formatting | bytes 5308416 | tf_op jit(solution)/shard_map/convert_element_type | solution.py:68
  99.9 84.1 %all_to_all.20 = bf16[64,16,1296]{2,1,0:T(8,128)(2,1)} all-to-all(bf16[64,16,1296]{2,1,0:T(8,128)(2,1)S(1)} %bitcast.48), channel_id=1, replica_groups=mesh['pts'=64,'bins'=12] {'pts'}, dimensions={0} | all-to-all | bytes 5308416 | tf_op jit(solution)/shard_map/all_to_all | solution.py:70
  184.0 4.4 %copy.25 = bf16[1,1,1024,1296]{2,3,1,0:T(8,128)(2,1)} copy(bf16[1,1,1024,1296]{3,2,1,0:T(8,128)(2,1)} %bitcast.49) | data formatting | bytes 5308416 | tf_op jit(solution)/shard_map/reshape | solution.py:71
  (12 shorter events, 0.1 us)
Async XLA Ops:
  0.0 17.0 %copy-start = (f32[1296,2]{0,1:T(2,128)S(1)}, f32[1296,2]{0,1:T(2,128)}, u32[]{:S(2)}) copy-start(f32[1296,2]{0,1:T(2,128)} %param.7) | copy-start | bytes 31108
  2.6 15.2 %collective-permute-start.1 = (bf16[108,1,1536]{2,0,1:T(8,128)(2,1)S(1)}, bf16[108,1,1536]{2,0,1:T(8,128)(2,1)S(1)}, u32[]{:S(2)}, u32[]{:S(2)}) collective-permute-start(bf16[108,1,1536]{2,0,1:T(8,128)(2,1)S(1)} %get-tuple-element.6), channel_id=1, source_target_pairs={{12,0},{24,12},{36,24},{48,36},{60,48},{72,60},{84,72},{96,84},{10... | collective-permute-start | bytes 995336 | tf_op jit(solution)/shard_map/ppermute | solution.py:15
  15.1 6.1 %collective-permute-start = (bf16[108,1,1536]{2,0,1:T(8,128)(2,1)S(1)}, bf16[108,1,1536]{2,0,1:T(8,128)(2,1)S(1)}, u32[]{:S(2)}, u32[]{:S(2)}) collective-permute-start(bf16[108,1,1536]{2,0,1:T(8,128)(2,1)S(1)} %get-tuple-element.5), channel_id=1, source_target_pairs={{0,12},{12,24},{24,36},{36,48},{48,60},{60,72},{72,84},{84,96},{96... | collective-permute-start | bytes 995336 | tf_op jit(solution)/shard_map/ppermute | solution.py:12
  23.7 9.2 %copy-start.1 = (s32[1,1,512,1]{2,3,1,0:T(1,128)S(1)}, s32[1,1,512,1]{2,3,1,0:T(1,128)}, u32[]{:S(2)}) copy-start(s32[1,1,512,1]{2,3,1,0:T(1,128)} %param.11) | copy-start | bytes 6148
  25.9 61.6 %all-to-all-start = ((bf16[108,4,1536]{0,1,2:T(4,128)(2,1)}), bf16[108,4,1536]{0,1,2:T(4,128)(2,1)S(1)}, u32[]{:S(2)}, u32[]{:S(2)}) async-start(bf16[108,4,1536]{0,1,2:T(4,128)(2,1)} %copy.21), calls=%async_computation | async-start | bytes 3145728 | tf_op jit(solution)/shard_map/all_to_all | solution.py:47
where the time goes:
time: 189 us; the launch traced here: 188 us
  blocking collectives  84.1 us (44%)
  waiting for transfers between devices  55.7 us (29%)
  starting transfers between devices  21.3 us (11%)
  local copies, waits for them, and re-layouts  12.3 us (7%)
  other arithmetic  7.52 us (4%)
  matrix products  7.37 us (4%)
    all_to_all x1, blocking collectives, local(): lax.all_to_all(outgoing, 'pts', split_axis=0, concat_axis=0, tiled=True)  84.1 us
    all_to_all x1, waiting for transfers between devices, local(): lax.all_to_all(moved, 'bins', split_axis=2, concat_axis=0, tiled=True)  52.4 us
    ppermute x1, starting transfers between devices, padded_2(): lax.ppermute(lax.slice_in_dim(block, 0, width, axis=dim), axis, backward)  12.4 us
    dot_general x1, matrix products, local(): jnp.dot(selector, updated, preferred_element_type=jnp.float32)  7.37 us
    all_to_all x1, starting transfers between devices, local(): lax.all_to_all(moved, 'bins', split_axis=2, concat_axis=0, tiled=True)  6.96 us
    reshape x1, local copies, waits for them, and re-layouts, local(): return received.reshape(1, 1, owners_count * capacity, all_bins)  4.44 us
  transfers between devices with their start and end apart: 3, of which 2 were waited for; matrix products, arithmetic and copies ran while one was open for 2% of the time, Pallas kernels for 0%

commit v1 on v0

v1 whole, which is shorter than its diff:
```python
import functools

import jax
import jax.numpy as jnp
from jax import lax
from jax.experimental import pallas as pl
from jax.experimental.pallas import tpu as pltpu
from jax.sharding import PartitionSpec as P

MESH = pl.DeviceIdType.MESH
BF16, F32 = jnp.bfloat16, jnp.float32
NT = (((1,), (1,)), ((), ()))
LANES = 128


def dot(a, b, dims=None):
    if dims is None:
        return jnp.dot(a, b, preferred_element_type=F32)
    return lax.dot_general(a, b, dims, preferred_element_type=F32)


def zigzag(count, step):
    return (count // 2 + ((step + 1) // 2) * (1 - 2 * (step % 2))) % count


def pts_peer(me, count, step):
    if count != 64:
        return (me + 1 + step) % count
    y = (me // 8 + zigzag(8, step // 8)) % 8
    x = ((me // 2) % 4 + zigzag(4, (step // 2) % 4)) % 4
    core = (me % 2 + 1 - step % 2) % 2
    return y * 8 + x * 2 + core


def bins_peer(me, count, step):
    return (me + zigzag(count, step)) % count


def round_bins(padded):
    sizes, at, out = [16], 16, [(0, 16)]
    while at < padded:
        size = min(32, padded - at)
        out.append((at, size))
        at += size
    return out


def kernel(dims, masked, courant, upwind, sea, owner, coupling, out, *scratch):
    np_, nb, lb, rounds, lon, lc, cap, slots, bins = dims
    nr = len(rounds)
    (hbuf, coef, sel, dbuf, acc, hss, hrs, zss, zrs, xss, xrs), rest = scratch[:11], scratch[11:]
    send, got, gath, recv, wmat, imat = [rest[k * nr:(k + 1) * nr] for k in range(6)]
    me = lax.axis_index("pts")
    mz = lax.axis_index("bins")
    up, down = (me + 1) % np_, (me + np_ - 1) % np_
    lat = masked.shape[2]
    pts = lon * lc
    tiles = 4
    mt = slots // tiles

    barrier = pltpu.get_barrier_semaphore()

    @pl.loop(0, np_ - 1)
    def _(k):
        pl.semaphore_signal(barrier, inc=1, device_id={"pts": pts_peer(me, np_, k)}, device_id_type=MESH)

    @pl.loop(0, nb - 1)
    def _(k):
        pl.semaphore_signal(barrier, inc=1, device_id={"bins": bins_peer(mz, nb, k)}, device_id_type=MESH)

    first = mz * lb
    rows = lax.broadcasted_iota(jnp.int32, (coef.shape[0], bins), 0)
    cols = lax.broadcasted_iota(jnp.int32, (coef.shape[0], bins), 1)
    pick = jnp.where((rows < lb) & (cols == rows + first), 1.0, 0.0).astype(F32)
    table = jnp.concatenate(
        [courant[...], upwind[...].astype(F32), jnp.zeros((4, bins), F32)], axis=0
    )
    coef[:, 0:8] = lax.dot_general(
        pick, table, NT, precision=lax.Precision.HIGHEST, preferred_element_type=F32
    )

    ids = lax.broadcasted_iota(jnp.int32, (np_, lc), 0)
    named = jnp.concatenate(
        [jnp.where(ids == owner[i:i + 1, :], 1.0, 0.0) for i in range(lon)], axis=1
    )
    before = lax.broadcasted_iota(jnp.int32, (pts, pts), 0)
    after = lax.broadcasted_iota(jnp.int32, (pts, pts), 1)
    upper = jnp.where(before <= after, 1.0, 0.0).astype(BF16)
    counts = dot(named.astype(BF16), upper)
    rank = jnp.sum(counts * named, axis=0, keepdims=True) - 1.0
    column = pl.multiple_of(mz * lc, LANES)
    for i in range(lon):
        slot = owner[i:i + 1, :].astype(F32) * float(cap) + rank[:, i * lc:(i + 1) * lc]
        weight = sea[i:i + 1, pl.ds(column, lc)].astype(F32)
        row = lax.broadcasted_iota(jnp.int32, (slots, lc), 0).astype(F32)
        sel[:, i * lc:(i + 1) * lc] = jnp.where(row == slot, weight, 0.0).astype(BF16)

    pl.semaphore_wait(barrier, np_ - 1 + nb - 1)

    for r, (q0, qn) in enumerate(rounds):
        for row, there, side in ((lon - 1, up, 0), (0, down, 1)):
            pltpu.make_async_remote_copy(
                src_ref=masked.at[row, pl.ds(q0, qn)],
                dst_ref=hbuf.at[side, pl.ds(q0, qn)],
                send_sem=hss.at[r],
                recv_sem=hrs.at[r],
                device_id={"pts": there},
                device_id_type=MESH,
            ).start()

    low_on = jnp.where(me > 0, 1.0, 0.0).astype(F32)
    high_on = jnp.where(me < np_ - 1, 1.0, 0.0).astype(F32)
    lane = lax.broadcasted_iota(jnp.int32, (16, lat), 1)
    for r, (q0, qn) in enumerate(rounds):
        span = pl.ds(q0, qn)
        pltpu.make_async_copy(hbuf.at[:, span], hbuf.at[:, span], hrs.at[r]).wait()
        for h in range(qn // 16):
            a0 = q0 + 16 * h
            at = pl.ds(a0, 16)
            cx, cy = coef[at, 0:1], coef[at, 1:2]
            ux, uy = coef[at, 2:3], coef[at, 3:4]
            lines = [hbuf[0, at, :].astype(F32) * low_on]
            lines += [masked[i, at, :].astype(F32) for i in range(lon)]
            lines += [hbuf[1, at, :].astype(F32) * high_on]
            for i in range(lon):
                center = lines[i + 1]
                donor_x = jnp.where(ux == 0.0, lines[i], lines[i + 2])
                lower = jnp.where(lane == 0, 0.0, pltpu.roll(center, 1, 1))
                higher = jnp.where(lane == lat - 1, 0.0, pltpu.roll(center, lat - 1, 1))
                donor_y = jnp.where(uy == 0.0, lower, higher)
                moved = center - cx * (center - donor_x) - cy * (center - donor_y)
                moved = (moved * sea[i:i + 1, :].astype(F32)).astype(BF16)
                for j in range(nb):
                    send[r][j, i, pl.ds(16 * h, 16), :] = moved[:, j * lc:(j + 1) * lc]

        @pl.loop(0, nb - 1)
        def _(k):
            there = bins_peer(mz, nb, k)
            pltpu.make_async_remote_copy(
                src_ref=send[r].at[there],
                dst_ref=got[r].at[mz],
                send_sem=zss.at[r],
                recv_sem=zrs.at[r],
                device_id={"bins": there},
                device_id_type=MESH,
            ).start()

        pltpu.make_async_copy(send[r].at[mz], got[r].at[mz], zrs.at[r]).start()

    def select(r):
        qn = rounds[r][1]
        pltpu.make_async_copy(send[r], got[r], zrs.at[r]).wait()
        width = nb * qn
        block = jnp.concatenate(
            [got[r][:, i].reshape(width, lc) for i in range(lon)], axis=1
        )

        @pl.loop(0, tiles)
        def _(m):
            part = sel[pl.ds(pl.multiple_of(m * mt, mt), mt), :]
            block = jnp.concatenate(
                [got[r][:, i].reshape(width, lc) for i in range(lon)], axis=1
            )
            rows = dot(part, block, NT).astype(BF16)
            gath[r][pl.ds(m * (np_ // tiles), np_ // tiles), :, 0:width] = rows.reshape(
                np_ // tiles, cap, width
            )

        @pl.loop(0, np_ - 1)
        def _(k):
            there = pts_peer(me, np_, k)
            pltpu.make_async_remote_copy(
                src_ref=gath[r].at[there],
                dst_ref=recv[r].at[me],
                send_sem=xss.at[r],
                recv_sem=xrs.at[r],
                device_id={"pts": there},
                device_id_type=MESH,
            ).start()

        pltpu.make_async_copy(gath[r].at[me], recv[r].at[me], xrs.at[r]).start()

    ot = dbuf.shape[1] // LANES

    def prepare(r):
        q0, qn = rounds[r]
        width = nb * qn
        full = wmat[r].shape[0]

        def bin_of(k):
            q = k % qn + q0
            return jnp.where(q < lb, (k // qn) * lb + q, -1)

        k = lax.broadcasted_iota(jnp.int32, (width, bins), 0)
        n = lax.broadcasted_iota(jnp.int32, (width, bins), 1)
        order = jnp.where(n == bin_of(k), 1.0, 0.0).astype(BF16)
        dbuf[0:width, 0:bins] = dot(order, coupling[...]).astype(BF16)
        if dbuf.shape[1] > bins:
            dbuf[0:width, bins:] = jnp.zeros((width, dbuf.shape[1] - bins), BF16)
        e0 = lax.broadcasted_iota(jnp.int32, (LANES, LANES), 0)
        e1 = lax.broadcasted_iota(jnp.int32, (LANES, LANES), 1)
        eye = jnp.where(e0 == e1, 1.0, 0.0).astype(BF16)
        for t in range(ot):
            wmat[r][t * LANES:(t + 1) * LANES, :] = dot(
                eye, dbuf[0:width, t * LANES:(t + 1) * LANES], NT
            ).astype(BF16)
        wmat[r][bins:bins + 8, :] = jnp.ones((8, width), BF16)
        n = lax.broadcasted_iota(jnp.int32, (full, width), 0)
        k = lax.broadcasted_iota(jnp.int32, (full, width), 1)
        imat[r][...] = jnp.where(n == bin_of(k), 1.0, 0.0).astype(BF16)

    def couple(r):
        width = nb * rounds[r][1]
        pltpu.make_async_copy(gath[r], recv[r], xrs.at[r]).wait()

        @pl.loop(0, tiles)
        def _(m):
            rows = recv[r][pl.ds(m * (np_ // tiles), np_ // tiles), :, 0:width].reshape(mt, width)
            total = dot(wmat[r][0:bins + 8, :], rows, NT) + dot(imat[r][0:bins + 8, :], rows, NT)
            if r > 0:
                total = total + acc[m]
            if r < nr - 1:
                acc[m] = total
            else:
                scale = 1.0 / (1.0 + total[bins:bins + 1, :] / float(bins))
                out[:, pl.ds(pl.multiple_of(m * mt, mt), mt)] = (total[0:bins] * scale).astype(BF16)

    select(0)
    for r in range(nr):
        prepare(r)
        if r + 1 < nr:
            select(r + 1)
    for r in range(nr):
        couple(r)
    for r, (q0, qn) in enumerate(rounds):
        span = pl.ds(q0, qn)
        pltpu.make_async_copy(hbuf.at[:, span], hbuf.at[:, span], hss.at[r]).wait()
        pltpu.make_async_copy(send[r].at[pl.ds(0, nb - 1)], got[r].at[pl.ds(0, nb - 1)], zss.at[r]).wait()
        pltpu.make_async_copy(gath[r].at[pl.ds(0, np_ - 1)], recv[r].at[pl.ds(0, np_ - 1)], xss.at[r]).wait()


def local(spectrum, courant, upwind, coupling, sea, owner):
    lb, lon, lat = spectrum.shape
    np_, nb = lax.axis_size("pts"), lax.axis_size("bins")
    bins = coupling.shape[0]
    lc = lat // nb
    pts = lon * lc
    cap = max(2, (2 * pts + np_ - 1) // np_)
    slots = np_ * cap
    padded = -(-lb // 16) * 16
    rounds = round_bins(padded)
    nr = len(rounds)
    masked = jnp.transpose(spectrum * sea.astype(BF16)[None], (1, 0, 2))
    masked = jnp.pad(masked, ((0, 0), (0, padded - lb), (0, 0)))
    wide = [-(-nb * q // LANES) * LANES for _, q in rounds]
    full = -(-(bins + 8) // LANES) * LANES
    dims = (np_, nb, lb, rounds, lon, lc, cap, slots, bins)
    scratch = [
        pltpu.VMEM((2, padded, lat), BF16),
        pltpu.VMEM((padded, LANES), F32),
        pltpu.VMEM((slots, pts), BF16),
        pltpu.VMEM((nb * 32, full), BF16),
        pltpu.VMEM((4, bins + 8, slots // 4), F32),
    ]
    scratch += [pltpu.SemaphoreType.DMA((nr,))] * 6
    scratch += [pltpu.VMEM((nb, lon, q, lc), BF16) for _, q in rounds] * 2
    scratch += [pltpu.VMEM((np_, cap, w), BF16) for w in wide] * 2
    scratch += [pltpu.VMEM((full, nb * q), BF16) for _, q in rounds] * 2
    vmem = pl.BlockSpec(memory_space=pltpu.VMEM)
    result = pl.pallas_call(
        functools.partial(kernel, dims),
        out_shape=jax.ShapeDtypeStruct((bins, slots), BF16),
        in_specs=[vmem] * 6,
        out_specs=vmem,
        scratch_shapes=scratch,
        compiler_params=pltpu.CompilerParams(
            collective_id=0, has_side_effects=True, vmem_limit_bytes=60 * 1024 * 1024
        ),
        name="wave_step",
    )(masked, courant.T, upwind.T, sea, owner.reshape(lon, lc), coupling)
    return result.T.reshape(1, 1, slots, bins)


def solution(mesh):
    placed = (P("bins", "pts", None), P(), P(), P(), P("pts", None), P("pts", "bins", None, None))
    return jax.shard_map(
        local, mesh=mesh, in_specs=placed, out_specs=P("pts", "bins", None, None), check_vma=False
    )
```

time: 189 us -> 119 us (0.63)
  Pallas kernels: 0 us -> 111 us
  blocking collectives: 84.1 us -> 0 us
  waiting for transfers between devices: 55.7 us -> 0 us
  starting transfers between devices: 21.3 us -> 0 us
  local copies, waits for them, and re-layouts: 12.3 us -> 4.69 us
  matrix products: 7.37 us -> 0 us
  other arithmetic: 7.52 us -> 2.5 us
    pallas_call x0 -> x1, Pallas kernels: none -> 111 us  [local(): pl.pallas_call(functools.partial(kernel, dims), out_shape=jax.ShapeDtypeS...]
    all_to_all x1 -> x0, blocking collectives: 84.1 us -> none  [local(): lax.all_to_all(outgoing, 'pts', split_axis=0, concat_axis=0, tiled=True)]
    all_to_all x1 -> x0, waiting for transfers between devices: 52.4 us -> none  [local(): lax.all_to_all(moved, 'bins', split_axis=2, concat_axis=0, tiled=True)]
    ppermute x2 -> x0, starting transfers between devices: 14.3 us -> none  [the longest x1 12.4 us: padded_2(): lax.ppermute(lax.slice_in_dim(block, 0, width, axis=dim), axis, backward)]
    dot_general x1 -> x0, matrix products: 7.37 us -> none  [local(): jnp.dot(selector, updated, preferred_element_type=jnp.float32)]
    all_to_all x1 -> x0, starting transfers between devices: 6.96 us -> none  [local(): lax.all_to_all(moved, 'bins', split_axis=2, concat_axis=0, tiled=True)]
    convert_element_type x2 -> x0, local copies, waits for them, and re-layouts: 5.52 us -> none  [the longest x1 3.27 us: local(): jnp.dot(selector, updated, preferred_element_type=jnp.float32)]
    reshape x1 -> x0, local copies, waits for them, and re-layouts: 4.44 us -> none  [local(): return received.reshape(1, 1, owners_count * capacity, all_bins)]
  transfers between devices with their start and end apart: 3 -> 0, of which waited for: 2 -> 0; matrix products, arithmetic and copies ran while one was open for 2% -> 0% of each run, Pallas kernels for 0% -> 0%
where the time goes in v1:
time: 119 us
  Pallas kernels  111 us (93%)
  local copies, waits for them, and re-layouts  4.69 us (4%)
  other arithmetic  2.5 us (2%)
    pallas_call x1, Pallas kernels, local(): pl.pallas_call(functools.partial(kernel, dims), out_shape=jax.ShapeDtypeS...  111 us
    unnamed x1, local copies, waits for them, and re-layouts  3.49 us

profile of v1, /device:TPU:1, one launch (start us, length us, event | category | flops | bytes accessed | tf_op | source)
XLA Modules:
  0.0 118.5 jit_solution(5972059223932590559)
XLA Ops:
  0.0 0.7 convert_element_type.5
  0.7 1.8 %fusion = bf16[4,108,1536]{2,1,0:T(8,128)(2,1)S(1)} fusion(bf16[108,4,1536]{2,1,0:T(4,128)(2,1)} %param.6, bf16[4,1536]{1,0:T(4,128)(2,1)S(1)} %convert_element_type.5), kind=kLoop, calls=%fused_computation.1 | loop fusion | flops 663552 | bytes 2666496 | tf_op jit(solution)/shard_map/transpose | solution.py:253
  2.5 1.2 %pad.4.masked = bf16[4,112,1536]{2,1,0:T(8,128)(2,1)} pad(bf16[4,108,1536]{2,1,0:T(8,128)(2,1)S(1)} %fusion, bf16[]{:T(256)} %constant.2.clone.1), padding=0_0x0_4x0_0 | pad | bytes 2703362 | tf_op jit(solution)/shard_map/jit(_pad)/pad | solution.py:254
  3.7 111.3 %wave_step.1 = bf16[1296,1024]{1,0:T(8,128)(2,1)} custom-call(bf16[4,112,1536]{2,1,0:T(8,128)(2,1)} %pad.4.masked, f32[2,1296]{1,0:T(2,128)} %bitcast.9, s32[2,1296]{1,0:T(2,128)} %bitcast.10, s32[4,1536]{1,0:T(4,128)} %sea.1, s32[4,128]{1,0:T(4,128)} %bitcast.11, bf16[1296,1296]{1,0:T(8,128)(2,1)} %coupling.1), custom_call_target="tpu_custom_call" | custom-call | tf_op jit(solution)/shard_map/wave_step/pallas_call | solution.py:270
  115.0 3.5 %copy.12 = bf16[1,1,1024,1296]{2,3,1,0:T(8,128)(2,1)} copy(bf16[1,1,1024,1296]{2,3,1,0:T(8,128)(2,1)} %bitcast.8) | data formatting | bytes 5308416

commit v2 on v0

v2 whole, which is shorter than its diff:
```python
import functools

import jax
import jax.numpy as jnp
from jax import lax
from jax.experimental import pallas as pl
from jax.experimental.pallas import tpu as pltpu
from jax.sharding import PartitionSpec as P

MESH = pl.DeviceIdType.MESH
BF16, F32 = jnp.bfloat16, jnp.float32
NT = (((1,), (1,)), ((), ()))
LANES = 128


def dot(a, b, dims=None):
    if dims is None:
        return jnp.dot(a, b, preferred_element_type=F32)
    return lax.dot_general(a, b, dims, preferred_element_type=F32)


def far_first(count):
    steps = [(count // 2 + ((k + 1) // 2) * (1 - 2 * (k % 2))) % count for k in range(count)]
    return [s for s in steps if s]


def near_first(count):
    return far_first(count)[::-1]


def each_peer(me, count, act):
    if count != 64:
        for d in range(1, count):
            act(lax.rem(me + d, count))
        return
    y, x, core = me // 8, lax.rem(me // 2, 4), lax.rem(me, 2)
    here = [
        lax.rem(x + dx, 4) * 2 + lax.rem(core + dc, 2)
        for dx in far_first(4) + [0]
        for dc in (1, 0)
    ]

    @pl.loop(0, 7)
    def _(k):
        row = lax.rem(y + 4 + ((k + 1) // 2) * (1 - 2 * lax.rem(k, 2)) + 8, 8) * 8
        for place in here:
            act(row + place)

    for place in here[:-1]:
        act(y * 8 + place)


def plan_chunks(blocks, size):
    total = (blocks - 1) * size
    cuts = [0]
    while cuts[-1] < total:
        left = total - cuts[-1]
        step = LANES // 2 if left <= LANES // 2 else LANES if left < 2 * LANES else 2 * LANES
        cuts.append(cuts[-1] + step)
    chunks = [([(0, 0, size)], LANES)]
    for a, b in zip(cuts[:-1], cuts[1:]):
        pieces, at = [], a
        while at < min(b, total):
            v, q = at // size + 1, at % size
            n = min(size - q, b - at)
            pieces.append((v, q, n))
            at += n
        chunks.append((pieces, b - a))
    return chunks


def kernel(dims, x, courant, upwind, sea, owner, table_hbm, out, *scratch):
    np_, nb, lb, padded, chunks, lon, lc, cap, slots, bins = dims
    nk = len(chunks)
    fixed, rest = scratch[:16], scratch[16:]
    edge, hbuf, coef, sel, dbuf, acc, send, got, coupling, hss, hrs, zss, zrs, xss, xrs, cs = fixed
    gath, recv, wmat = [rest[k * nk:(k + 1) * nk] for k in range(3)]
    me = lax.axis_index("pts")
    mz = lax.axis_index("bins")
    up, down = lax.rem(me + 1, np_), lax.rem(me + np_ - 1, np_)
    lat = x.shape[2]
    pts = lon * lc
    tiles = 4
    mt = slots // tiles
    own_tiles = np_ // tiles
    full = dbuf.shape[1]
    half = LANES // 2
    distances = [0] + near_first(nb)
    groups = [(a, min(16, lb - a)) for a in range(0, padded, 16)]
    rounds = [groups[a:a + 2] for a in range(0, len(groups), 2)]

    barrier = pltpu.get_barrier_semaphore()

    def greet(peer):
        pl.semaphore_signal(barrier, inc=1, device_id={"pts": peer}, device_id_type=MESH)

    each_peer(me, np_, greet)
    for d in distances[1:]:
        pl.semaphore_signal(
            barrier, inc=1, device_id={"bins": lax.rem(mz + d, nb)}, device_id_type=MESH
        )

    for side, row in ((0, lon - 1), (1, 0)):
        edge[side, 0:lb, :] = x[row] * sea[row:row + 1, :].astype(BF16)
        if padded > lb:
            edge[side, lb:padded, :] = jnp.zeros((padded - lb, lat), BF16)
    if padded > lb:
        for j in range(nb):
            for i in range(lon):
                send[j, i, lb:padded, :] = jnp.zeros((padded - lb, lc), BF16)

    low_on = jnp.where(me > 0, 1.0, 0.0).astype(F32)
    high_on = jnp.where(me < np_ - 1, 1.0, 0.0).astype(F32)

    def line(i, a, n):
        if i < 0:
            return hbuf[0, a:a + n, :].astype(F32) * low_on
        if i == lon:
            return hbuf[1, a:a + n, :].astype(F32) * high_on
        return x[i, a:a + n, :].astype(F32) * sea[i:i + 1, :].astype(F32)

    def advect(i, a, n):
        cx, cy = coef[a:a + n, 0:1], coef[a:a + n, 1:2]
        ux, uy = coef[a:a + n, 2:3], coef[a:a + n, 3:4]
        lane = lax.broadcasted_iota(jnp.int32, (n, lat), 1)
        center = line(i, a, n)
        donor_x = jnp.where(ux == 0.0, line(i - 1, a, n), line(i + 1, a, n))
        lower = jnp.where(lane == 0, 0.0, pltpu.roll(center, 1, 1))
        higher = jnp.where(lane == lat - 1, 0.0, pltpu.roll(center, lat - 1, 1))
        donor_y = jnp.where(uy == 0.0, lower, higher)
        moved = center - cx * (center - donor_x) - cy * (center - donor_y)
        moved = (moved * sea[i:i + 1, :].astype(F32)).astype(BF16)
        for j in range(nb):
            send[j, i, a:a + n, :] = moved[:, j * lc:(j + 1) * lc]

    pl.semaphore_wait(barrier, np_ - 1 + nb - 1)

    spans = [pl.ds(g[0][0], sum(16 for _ in g)) for g in rounds]
    for r, span in enumerate(spans):
        for side, there in ((0, up), (1, down)):
            pltpu.make_async_remote_copy(
                src_ref=edge.at[side, span],
                dst_ref=hbuf.at[side, span],
                send_sem=hss.at[r],
                recv_sem=hrs.at[r],
                device_id={"pts": there},
                device_id_type=MESH,
            ).start()
    load = pltpu.make_async_copy(table_hbm, coupling, cs.at[0])
    load.start()
    first = mz * lb
    rows = lax.broadcasted_iota(jnp.int32, (padded, bins), 0)
    cols = lax.broadcasted_iota(jnp.int32, (padded, bins), 1)
    pick = jnp.where((rows < lb) & (cols == rows + first), 1.0, 0.0).astype(F32)
    table = jnp.concatenate(
        [courant[...], upwind[...].astype(F32), jnp.zeros((4, bins), F32)], axis=0
    )
    coef[:, 0:8] = lax.dot_general(
        pick, table, NT, precision=lax.Precision.HIGHEST, preferred_element_type=F32
    )

    ids = lax.broadcasted_iota(jnp.int32, (np_, lc), 0)
    named = jnp.concatenate(
        [jnp.where(ids == owner[i:i + 1, :], 1.0, 0.0) for i in range(lon)], axis=1
    )
    before = lax.broadcasted_iota(jnp.int32, (pts, pts), 0)
    after = lax.broadcasted_iota(jnp.int32, (pts, pts), 1)
    upper = jnp.where(before <= after, 1.0, 0.0).astype(BF16)
    counts = dot(named.astype(BF16), upper)
    rank = jnp.sum(counts * named, axis=0, keepdims=True) - 1.0
    column = pl.multiple_of(mz * lc, LANES)
    for i in range(lon):
        slot = owner[i:i + 1, :].astype(F32) * float(cap) + rank[:, i * lc:(i + 1) * lc]
        weight = sea[i:i + 1, pl.ds(column, lc)].astype(F32)
        row = lax.broadcasted_iota(jnp.int32, (slots, lc), 0).astype(F32)
        sel[:, i * lc:(i + 1) * lc] = jnp.where(row == slot, weight, 0.0).astype(BF16)

    for a, n in groups:
        for i in range(1, lon - 1):
            advect(i, a, n)

    def pass_on(v, span):
        there = lax.rem(mz + distances[v], nb)
        pltpu.make_async_remote_copy(
            src_ref=send.at[there, :, span],
            dst_ref=got.at[v, :, span],
            send_sem=zss.at[v],
            recv_sem=zrs.at[v],
            device_id={"bins": there},
            device_id_type=MESH,
        ).start()

    near = min(2, nb - 1)
    for r, span in enumerate(spans):
        pltpu.make_async_copy(hbuf.at[:, span], hbuf.at[:, span], hrs.at[r]).wait()
        for a, n in rounds[r]:
            advect(0, a, n)
            advect(lon - 1, a, n)
        for v in range(1, near + 1):
            pass_on(v, span)
    for v in range(near + 1, nb):
        pass_on(v, slice(None))

    here = [False] * nb

    def select(c):
        pieces, width = chunks[c]
        for v, _, _ in pieces:
            if v and not here[v]:
                here[v] = True
                pltpu.make_async_copy(got.at[v], got.at[v], zrs.at[v]).wait()

        def column_of(i):
            parts = [
                (got[v, i, q:q + n, :] if v else send[mz, i, q:q + n, :]) for v, q, n in pieces
            ]
            spare = width - sum(n for _, _, n in pieces)
            if spare:
                parts.append(jnp.zeros((spare, lc), BF16))
            if width == half:
                parts = parts + parts
            return parts[0] if len(parts) == 1 else jnp.concatenate(parts, axis=0)

        @pl.loop(0, tiles)
        def _(m):
            part = sel[pl.ds(pl.multiple_of(m * mt, mt), mt), :]
            block = jnp.concatenate([column_of(i) for i in range(lon)], axis=1)
            wide = max(width, LANES)
            rows = dot(part, block, NT).reshape(own_tiles, cap, wide)
            if width == half:
                left = lax.broadcasted_iota(jnp.int32, (own_tiles, cap // 2, wide), 2) < half
                rows = jnp.where(left, rows[:, :cap // 2], rows[:, cap // 2:])
            gath[c][pl.ds(m * own_tiles, own_tiles)] = rows.astype(BF16)

        def push(peer):
            pltpu.make_async_remote_copy(
                src_ref=gath[c].at[peer],
                dst_ref=recv[c].at[me],
                send_sem=xss.at[c],
                recv_sem=xrs.at[c],
                device_id={"pts": peer},
                device_id_type=MESH,
            ).start()

        each_peer(me, np_, push)
        pltpu.make_async_copy(gath[c].at[me], recv[c].at[me], xrs.at[c]).start()

    def bin_of(k, c):
        pieces, width = chunks[c]
        if width == half:
            k = jnp.where(k < half, k, k - half)
        at, result = 0, jnp.full(k.shape, -1, jnp.int32)
        for v, q, n in pieces:
            block = lax.rem(mz + nb - distances[v], nb) * lb
            inside = (k >= at) & (k < at + min(n, lb - q))
            result = jnp.where(inside, block + q - at + k, result)
            at += n
        return result

    def prepare(c):
        width = max(chunks[c][1], LANES)
        k = lax.broadcasted_iota(jnp.int32, (width, bins), 0)
        n = lax.broadcasted_iota(jnp.int32, (width, bins), 1)
        order = jnp.where(n == bin_of(k, c), 1.0, 0.0).astype(BF16)
        dbuf[0:width, 0:bins] = dot(order, coupling[...]).astype(BF16)
        if full > bins:
            dbuf[0:width, bins:] = jnp.zeros((width, full - bins), BF16)
        e0 = lax.broadcasted_iota(jnp.int32, (LANES, LANES), 0)
        e1 = lax.broadcasted_iota(jnp.int32, (LANES, LANES), 1)
        eye = jnp.where(e0 == e1, 1.0, 0.0).astype(BF16)
        for t in range(full // LANES):
            wmat[c][t * LANES:(t + 1) * LANES, 0:width] = dot(
                eye, dbuf[0:width, t * LANES:(t + 1) * LANES], NT
            ).astype(BF16)
        wmat[c][bins:bins + 8, 0:width] = jnp.ones((8, width), BF16)
        n = lax.broadcasted_iota(jnp.int32, (full, width), 0)
        k = lax.broadcasted_iota(jnp.int32, (full, width), 1)
        wmat[c][:, width:] = jnp.where(n == bin_of(k, c), 1.0, 0.0).astype(BF16)

    def couple(c):
        pltpu.make_async_copy(gath[c], recv[c], xrs.at[c]).wait()
        width = max(chunks[c][1], LANES)

        @pl.loop(0, tiles)
        def _(m):
            rows = recv[c][pl.ds(m * own_tiles, own_tiles)]
            if chunks[c][1] == half:
                left = lax.broadcasted_iota(jnp.int32, rows.shape, 2) < half
                none = jnp.zeros_like(rows)
                rows = jnp.concatenate(
                    [jnp.where(left, rows, none), jnp.where(left, none, rows)], axis=1
                )
            rows = rows.reshape(mt, width)
            if width == LANES:
                rows = jnp.concatenate([rows, rows], axis=1)
                total = dot(wmat[c][0:bins + 8, :], rows, NT)
            else:
                total = dot(wmat[c][0:bins + 8, 0:width], rows, NT)
                total = total + dot(wmat[c][0:bins + 8, width:], rows, NT)
            if c > 0:
                total = total + acc[m]
            if c < nk - 1:
                acc[m] = total
            else:
                scale = 1.0 / (1.0 + total[bins:bins + 1, :] / float(bins))
                out[:, pl.ds(pl.multiple_of(m * mt, mt), mt)] = (total[0:bins] * scale).astype(BF16)

    select(0)
    select(1)
    load.wait()
    prepare(0)
    prepare(1)
    for c in range(2, nk):
        select(c)
        prepare(c)
        couple(c - 2)
    couple(nk - 2)
    couple(nk - 1)
    for r, span in enumerate(spans):
        pltpu.make_async_copy(edge.at[:, span], hbuf.at[:, span], hss.at[r]).wait()
    for v in range(1, nb):
        pltpu.make_async_copy(send.at[v], got.at[v], zss.at[v]).wait()
    for c in range(nk):
        pltpu.make_async_copy(
            gath[c].at[pl.ds(0, np_ - 1)], recv[c].at[pl.ds(0, np_ - 1)], xss.at[c]
        ).wait()


def local(spectrum, courant, upwind, coupling, sea, owner):
    lb, lon, lat = spectrum.shape
    np_, nb = lax.axis_size("pts"), lax.axis_size("bins")
    bins = coupling.shape[0]
    lc = lat // nb
    pts = lon * lc
    cap = max(2, (2 * pts + np_ - 1) // np_)
    slots = np_ * cap
    padded = -(-lb // 16) * 16
    chunks = plan_chunks(nb, lb)
    nk = len(chunks)
    full = -(-(bins + 8) // LANES) * LANES
    dims = (np_, nb, lb, padded, chunks, lon, lc, cap, slots, bins)
    most = max(LANES, max(w for _, w in chunks))
    scratch = [
        pltpu.VMEM((2, padded, lat), BF16),
        pltpu.VMEM((2, padded, lat), BF16),
        pltpu.VMEM((padded, LANES), F32),
        pltpu.VMEM((slots, pts), BF16),
        pltpu.VMEM((most, full), BF16),
        pltpu.VMEM((4, bins + 8, slots // 4), F32),
        pltpu.VMEM((nb, lon, padded, lc), BF16),
        pltpu.VMEM((nb, lon, padded, lc), BF16),
        pltpu.VMEM((bins, bins), BF16),
    ]
    counts = [-(-padded // 32)] * 2 + [nb] * 2 + [nk] * 2 + [1]
    scratch += [pltpu.SemaphoreType.DMA((n,)) for n in counts]
    packed = [(np_, cap if w >= LANES else cap // 2, max(w, LANES)) for _, w in chunks]
    scratch += [pltpu.VMEM(s, BF16) for s in packed] * 2
    scratch += [pltpu.VMEM((full, 2 * max(w, LANES)), BF16) for _, w in chunks]
    vmem = pl.BlockSpec(memory_space=pltpu.VMEM)
    result = pl.pallas_call(
        functools.partial(kernel, dims),
        out_shape=jax.ShapeDtypeStruct((bins, slots), BF16),
        in_specs=[vmem] * 5 + [pl.BlockSpec(memory_space=pltpu.HBM)],
        out_specs=vmem,
        scratch_shapes=scratch,
        compiler_params=pltpu.CompilerParams(
            collective_id=0, has_side_effects=True, vmem_limit_bytes=50 * 1024 * 1024
        ),
        name="wave_step",
    )(jnp.transpose(spectrum, (1, 0, 2)), courant.T, upwind.T, sea, owner.reshape(lon, lc), coupling)
    return result.T.reshape(1, 1, slots, bins)


def solution(mesh):
    placed = (P("bins", "pts", None), P(), P(), P(), P("pts", None), P("pts", "bins", None, None))
    return jax.shard_map(
        local, mesh=mesh, in_specs=placed, out_specs=P("pts", "bins", None, None), check_vma=False
    )
```

time: 189 us -> 99.8 us (0.53)
  Pallas kernels: 0 us -> 95.5 us
  blocking collectives: 84.1 us -> 0 us
  waiting for transfers between devices: 55.7 us -> 0 us
  starting transfers between devices: 21.3 us -> 0 us
  local copies, waits for them, and re-layouts: 12.3 us -> 3.11 us
  other arithmetic: 7.52 us -> 0 us
  matrix products: 7.37 us -> 0 us
    pallas_call x0 -> x1, Pallas kernels: none -> 95.5 us  [local(): pl.pallas_call(functools.partial(kernel, dims), out_shape=jax.ShapeDtypeS...]
    all_to_all x1 -> x0, blocking collectives: 84.1 us -> none  [local(): lax.all_to_all(outgoing, 'pts', split_axis=0, concat_axis=0, tiled=True)]
    all_to_all x1 -> x0, waiting for transfers between devices: 52.4 us -> none  [local(): lax.all_to_all(moved, 'bins', split_axis=2, concat_axis=0, tiled=True)]
    ppermute x2 -> x0, starting transfers between devices: 14.3 us -> none  [the longest x1 12.4 us: padded_2(): lax.ppermute(lax.slice_in_dim(block, 0, width, axis=dim), axis, backward)]
    dot_general x1 -> x0, matrix products: 7.37 us -> none  [local(): jnp.dot(selector, updated, preferred_element_type=jnp.float32)]
    all_to_all x1 -> x0, starting transfers between devices: 6.96 us -> none  [local(): lax.all_to_all(moved, 'bins', split_axis=2, concat_axis=0, tiled=True)]
    convert_element_type x2 -> x0, local copies, waits for them, and re-layouts: 5.52 us -> none  [the longest x1 3.27 us: local(): jnp.dot(selector, updated, preferred_element_type=jnp.float32)]
    reshape x1 -> x0, local copies, waits for them, and re-layouts: 4.44 us -> none  [local(): return received.reshape(1, 1, owners_count * capacity, all_bins)]
  transfers between devices with their start and end apart: 3 -> 0, of which waited for: 2 -> 0; matrix products, arithmetic and copies ran while one was open for 2% -> 0% of each run, Pallas kernels for 0% -> 0%
where the time goes in v2:
time: 99.8 us; the launch traced here: 98.6 us
  Pallas kernels  95.5 us (96%)
  local copies, waits for them, and re-layouts  3.11 us (3%)
    pallas_call x1, Pallas kernels, local(): pl.pallas_call(functools.partial(kernel, dims), out_shape=jax.ShapeDtypeS...  95.5 us
    unnamed x10, local copies, waits for them, and re-layouts  3.11 us

profile of v2, /device:TPU:1, one launch (start us, length us, event | category | flops | bytes accessed | tf_op | source)
XLA Modules:
  0.0 98.6 jit_solution(8696423224860901831)
XLA Ops:
  0.0 0.0 copy-start.3
  0.0 0.0 copy-start
  0.0 0.0 copy-start.2
  0.0 0.0 copy-start.1
  0.0 1.6 %copy.9 = bf16[108,4,1536]{2,0,1:T(8,128)(2,1)S(1)} copy(bf16[108,4,1536]{2,1,0:T(4,128)(2,1)} %param.6) | data formatting | bytes 2654208 | tf_op args[0]
  1.6 0.0 copy-done.3
  1.6 0.0 copy-done
  1.6 0.0 copy-done.2
  1.6 0.0 copy-done.1
  1.7 95.5 %wave_step.1 = bf16[1296,1024]{1,0:T(8,128)(2,1)S(1)} custom-call(bf16[4,108,1536]{2,1,0:T(8,128)(2,1)S(1)} %bitcast.10, f32[2,1296]{1,0:T(2,128)S(1)} %bitcast.11, s32[2,1296]{1,0:T(2,128)S(1)} %bitcast.12, s32[4,1536]{1,0:T(4,128)S(1)} %copy-done, s32[4,128]{1,0:T(4,128)S(1)} %bitcast.13, bf16[1296,1296]{1,0:T(8,128)(2,1)} %table_hbm.1), custom_call_target="tpu_custom_call" | custom-call | tf_op jit(solution)/shard_map/wave_step/pallas_call | solution.py:360
  97.1 1.5 %copy.11 = bf16[1,1,1024,1296]{2,3,1,0:T(8,128)(2,1)} copy(bf16[1,1,1024,1296]{2,3,1,0:T(8,128)(2,1)S(1)} %bitcast.9) | data formatting | bytes 5308416
Async XLA Ops:
  0.0 1.6 %copy-start.3 = (s32[1,1,512,1]{2,3,1,0:T(1,128)S(1)}, s32[1,1,512,1]{2,3,1,0:T(1,128)}, u32[]{:S(2)}) copy-start(s32[1,1,512,1]{2,3,1,0:T(1,128)} %param.11) | copy-start | bytes 6148
  0.0 1.6 %copy-start = (s32[4,1536]{1,0:T(4,128)S(1)}, s32[4,1536]{1,0:T(4,128)}, u32[]{:S(2)}) copy-start(s32[4,1536]{1,0:T(4,128)} %sea.1) | copy-start | bytes 73732
  0.0 1.6 %copy-start.2 = (s32[1296,2]{0,1:T(2,128)S(1)}, s32[1296,2]{0,1:T(2,128)}, u32[]{:S(2)}) copy-start(s32[1296,2]{0,1:T(2,128)} %param.8) | copy-start | bytes 31108
  0.0 1.6 %copy-start.1 = (f32[1296,2]{0,1:T(2,128)S(1)}, f32[1296,2]{0,1:T(2,128)}, u32[]{:S(2)}) copy-start(f32[1296,2]{0,1:T(2,128)} %param.7) | copy-start | bytes 31108

commit v3 on v2

--- a/solution.py
+++ b/solution.py
@@ -51,11 +51,11 @@
 
 
 def plan_chunks(blocks, size):
-    total = (blocks - 1) * size
+    total = (blocks - 2) * size
     cuts = [0]
     while cuts[-1] < total:
         left = total - cuts[-1]
-        step = LANES // 2 if left <= LANES // 2 else LANES if left < 2 * LANES else 2 * LANES
+        step = LANES // 2 if left <= LANES // 2 else LANES if left < 2 * LANES or len(cuts) < 3 else 2 * LANES
         cuts.append(cuts[-1] + step)
     chunks = [([(0, 0, size)], LANES)]
     for a, b in zip(cuts[:-1], cuts[1:]):
@@ -66,7 +66,7 @@
             pieces.append((v, q, n))
             at += n
         chunks.append((pieces, b - a))
-    return chunks
+    return chunks + [([(blocks - 1, 0, size)], LANES)]
 
 
 def kernel(dims, x, courant, upwind, sea, owner, table_hbm, out, *scratch):
@@ -307,12 +307,15 @@
 
     select(0)
     select(1)
+    select(2)
     load.wait()
-    prepare(0)
-    prepare(1)
-    for c in range(2, nk):
+    for c in range(3):
+        prepare(c)
+    for c in range(3, nk):
         select(c)
         prepare(c)
+        if c == 3:
+            couple(0)
         couple(c - 2)
     couple(nk - 2)
     couple(nk - 1)

time: 99.8 us -> 98.6 us (0.988); the launches traced: 98.6 us -> 98.5 us
  no operation moved by 1% of the time
where the time goes in v3:
time: 98.6 us; the launch traced here: 98.5 us
  Pallas kernels  95.3 us (97%)
  local copies, waits for them, and re-layouts  3.11 us (3%)
    pallas_call x1, Pallas kernels, local(): pl.pallas_call(functools.partial(kernel, dims), out_shape=jax.ShapeDtypeS...  95.3 us
    unnamed x10, local copies, waits for them, and re-layouts  3.11 us

profile of v3, /device:TPU:1, one launch (start us, length us, event | category | flops | bytes accessed | tf_op | source)
XLA Modules:
  0.0 98.5 jit_solution(11165049244480853378)
XLA Ops:
  0.0 0.0 copy-start.3
  0.0 0.0 copy-start
  0.0 0.0 copy-start.2
  0.0 0.0 copy-start.1
  0.0 1.6 %copy.9 = bf16[108,4,1536]{2,0,1:T(8,128)(2,1)S(1)} copy(bf16[108,4,1536]{2,1,0:T(4,128)(2,1)} %param.6) | data formatting | bytes 2654208 | tf_op args[0]
  1.6 0.0 copy-done.3
  1.6 0.0 copy-done
  1.6 0.0 copy-done.2
  1.6 0.0 copy-done.1
  1.7 95.3 %wave_step.1 = bf16[1296,1024]{1,0:T(8,128)(2,1)S(1)} custom-call(bf16[4,108,1536]{2,1,0:T(8,128)(2,1)S(1)} %bitcast.10, f32[2,1296]{1,0:T(2,128)S(1)} %bitcast.11, s32[2,1296]{1,0:T(2,128)S(1)} %bitcast.12, s32[4,1536]{1,0:T(4,128)S(1)} %copy-done, s32[4,128]{1,0:T(4,128)S(1)} %bitcast.13, bf16[1296,1296]{1,0:T(8,128)(2,1)} %table_hbm.1), custom_call_target="tpu_custom_call" | custom-call | tf_op jit(solution)/shard_map/wave_step/pallas_call | solution.py:363
  97.0 1.5 %copy.11 = bf16[1,1,1024,1296]{2,3,1,0:T(8,128)(2,1)} copy(bf16[1,1,1024,1296]{2,3,1,0:T(8,128)(2,1)S(1)} %bitcast.9) | data formatting | bytes 5308416
Async XLA Ops:
  0.0 1.6 %copy-start.3 = (s32[1,1,512,1]{2,3,1,0:T(1,128)S(1)}, s32[1,1,512,1]{2,3,1,0:T(1,128)}, u32[]{:S(2)}) copy-start(s32[1,1,512,1]{2,3,1,0:T(1,128)} %param.11) | copy-start | bytes 6148
  0.0 1.6 %copy-start = (s32[4,1536]{1,0:T(4,128)S(1)}, s32[4,1536]{1,0:T(4,128)}, u32[]{:S(2)}) copy-start(s32[4,1536]{1,0:T(4,128)} %sea.1) | copy-start | bytes 73732
  0.0 1.6 %copy-start.2 = (s32[1296,2]{0,1:T(2,128)S(1)}, s32[1296,2]{0,1:T(2,128)}, u32[]{:S(2)}) copy-start(s32[1296,2]{0,1:T(2,128)} %param.8) | copy-start | bytes 31108
  0.0 1.6 %copy-start.1 = (f32[1296,2]{0,1:T(2,128)S(1)}, f32[1296,2]{0,1:T(2,128)}, u32[]{:S(2)}) copy-start(f32[1296,2]{0,1:T(2,128)} %param.7) | copy-start | bytes 31108
